TPU v7x, 128 devices: a whole 4x4x4 slice. The times are simulated.
128 devices in a mesh: req: 16 (over y, x), mlp: 8 (over z, core).
Axes of the slice: x: 4, y: 4, z: 4, core: 2. Of those that a mesh axis runs over, the one named last changes fastest.
Arguments:
- tokens: bfloat16 [16384, 1024], P(('req', 'mlp')), may hold values from -6 to 6
- token_owner: int32 [16384, 1], replicated, may hold values from 0 to 127; in each aligned block of 128 rows (0 to 127, 128 to 255, ...) at most 2 rows name the same one
- token_request: int32 [16384], replicated, may hold values from 0 to 3
- cache_len: int32 [512], P(('req', 'mlp')), may hold values from 1 to 512, 131072 in all
- cache_k: bfloat16 [512, 512, 1024], P(('req', 'mlp')), may hold values from -6 to 6
- cache_v: bfloat16 [512, 512, 1024], P(('req', 'mlp')), may hold values from -12 to 12
- w_qkv: bfloat16 [1024, 3072], replicated, may hold values from -0.1875 to 0.1875
- w_out: bfloat16 [1024, 1024], replicated, may hold values from -0.375 to 0.375
- w_fc1: bfloat16 [1024, 4096], P(None, 'mlp'), may hold values from -0.1875 to 0.1875
- w_fc2: bfloat16 [4096, 1024], P('mlp'), may hold values from -0.09375 to 0.09375
- ln1_gain: float32 [1024], replicated, may hold values from 0.1 to 1.9
- ln1_bias: float32 [1024], replicated, may hold values from -3 to 3
- ln2_gain: float32 [1024], replicated, may hold values from 0.1 to 1.9
- ln2_bias: float32 [1024], replicated, may hold values from -3 to 3
Outputs:
- layer_out: bfloat16 [16384, 1024], P(('req', 'mlp'))
Inputs may be any that keep to these rules, and one draw needn't show every extreme that they name: `token_owner`: in each aligned block of 128 rows (the rows of one device) no owner is named more than 2 times, a bound that some block reaches; every owner is named somewhere. `cache_len`: some request has exactly 512 cached positions.
All inputs are finite; a program needn't handle non-finite values. No bound on the sum of `cache_len` on one device may be relied on, other than what follows from the above.
Results may differ from a plain program's by a relative error of at most 0.01.
Values may be sent and summed in bfloat16 or wider, within the bound.
A program may use at most 128 MiB of HBM per device.

v0:
```python
import jax
import jax.numpy as jnp
from jax import lax
from jax.sharding import PartitionSpec as P

HEADS = 16
epsilon = 1e-05


def layer_norm(values, gain, shift):
    center = values - jnp.mean(values, axis=-1, keepdims=True)
    spread = jnp.mean(center * center, axis=-1, keepdims=True)
    return center * lax.rsqrt(spread + epsilon) * gain + shift


def slot_table(owners_flat, requests_flat, owner_index, devices, tok_dev, capacity):
    owners = owners_flat.reshape(devices, tok_dev)
    requests = requests_flat.reshape(devices, tok_dev)
    mine_mask = (owners == owner_index).astype(jnp.int32)
    ranking = jnp.cumsum(mine_mask, axis=1) - 1
    places = jnp.arange(capacity, dtype=jnp.int32)
    hit_table = mine_mask[:, :, None] * (ranking[:, :, None] == places[None, None, :]).astype(
        jnp.int32
    )
    filled = jnp.sum(hit_table, axis=1)
    positions = jnp.arange(tok_dev, dtype=jnp.int32)
    local_row = jnp.sum(hit_table * positions[None, :, None], axis=1)
    sources = jnp.arange(devices, dtype=jnp.int32)[:, None]
    global_row = jnp.where(filled > 0, sources * tok_dev + local_row, -1).reshape(-1)
    slot_request = jnp.sum(hit_table * requests[:, :, None], axis=1).reshape(-1)
    return (global_row, slot_request, filled.reshape(-1))


def attend(projections, cache_keys, cache_values, lengths, global_row, slot_request, filled):
    slot_count = projections.shape[0]
    width = projections.shape[1] // 3
    head_dim = width // HEADS
    context = cache_keys.shape[1]
    score_scale = head_dim ** (-0.5)
    queries = projections[:, :width].reshape(slot_count, HEADS, head_dim)
    key_new = projections[:, width : 2 * width].reshape(slot_count, HEADS, head_dim)
    value_new = projections[:, 2 * width :].reshape(slot_count, HEADS, head_dim)
    new_mask = (
        (filled[None, :] > 0)
        & (slot_request[None, :] == slot_request[:, None])
        & (global_row[None, :] <= global_row[:, None])
    )
    new_score = (
        jnp.einsum("rhd,shd->hrs", queries, key_new, preferred_element_type=jnp.float32)
        * score_scale
    )
    new_exp = jnp.where(new_mask[None], jnp.exp(new_score), jnp.float32(0.0))
    new_total = jnp.sum(new_exp, axis=-1)
    key_place = jnp.arange(context, dtype=jnp.int32)

    def one_request(items):
        keys_here, values_here, length, request_index = items
        mask = (slot_request[:, None] == request_index) & (key_place[None, :] < length)
        score = (
            jnp.einsum(
                "rhd,khd->hrk",
                queries,
                keys_here.reshape(context, HEADS, head_dim),
                preferred_element_type=jnp.float32,
            )
            * score_scale
        )
        old_exp = jnp.where(mask[None], jnp.exp(score), jnp.float32(0.0))
        old_total = jnp.sum(old_exp, axis=-1)
        total = old_total + new_total
        total = jnp.where(total > 0, total, jnp.float32(1.0))
        weight = (old_exp / total[:, :, None]).astype(jnp.bfloat16)
        part = jnp.einsum(
            "hrk,khd->rhd",
            weight,
            values_here.reshape(context, HEADS, head_dim),
            preferred_element_type=jnp.float32,
        )
        return (part, old_total)

    request_ids = jnp.arange(cache_keys.shape[0], dtype=jnp.int32)
    parts, totals = lax.map(one_request, (cache_keys, cache_values, lengths, request_ids))
    denominator = jnp.sum(totals, axis=0) + new_total
    denominator = jnp.where(denominator > 0, denominator, jnp.float32(1.0))
    new_weight = (new_exp / denominator[:, :, None]).astype(jnp.bfloat16)
    result = jnp.sum(parts, axis=0)
    result = result + jnp.einsum(
        "hrs,shd->rhd", new_weight, value_new, preferred_element_type=jnp.float32
    )
    return result.reshape(slot_count, width).astype(jnp.bfloat16)


def per_device(
    tokens,
    token_owner,
    token_request,
    cache_len,
    cache_k,
    cache_v,
    w_qkv,
    w_out,
    w_fc1,
    w_fc2,
    ln1_gain,
    ln1_bias,
    ln2_gain,
    ln2_bias,
):
    n_req = lax.axis_size("req")
    n_mlp = lax.axis_size("mlp")
    devices = n_req * n_mlp
    owner_index = lax.axis_index("req") * n_mlp + lax.axis_index("mlp")
    tok_dev, width = tokens.shape
    capacity = max(2, 2 * tok_dev // devices)
    slot_count = devices * capacity
    owners_flat = token_owner.reshape(-1)
    my_owners = lax.dynamic_slice_in_dim(owners_flat, owner_index * tok_dev, tok_dev)
    owner_onehot = (my_owners[:, None] == jnp.arange(devices, dtype=jnp.int32)[None, :]).astype(
        jnp.int32
    )
    ranking = jnp.cumsum(owner_onehot, axis=0) - 1
    my_rank = jnp.sum(owner_onehot * ranking, axis=1)
    column = my_owners * capacity + my_rank
    dispatch = (column[:, None] == jnp.arange(slot_count, dtype=jnp.int32)[None, :]).astype(
        jnp.bfloat16
    )
    outgoing = jnp.einsum("tr,td->rd", dispatch, tokens, preferred_element_type=jnp.float32).astype(
        jnp.bfloat16
    )
    arrived = lax.all_to_all(
        outgoing.reshape(devices, capacity, width),
        ("req", "mlp"),
        split_axis=0,
        concat_axis=0,
        tiled=True,
    )
    projections = jnp.dot(
        arrived.reshape(slot_count, width), w_qkv, preferred_element_type=jnp.float32
    ).astype(jnp.bfloat16)
    global_row, slot_request, filled = slot_table(
        owners_flat, token_request, owner_index, devices, tok_dev, capacity
    )
    attended = attend(projections, cache_k, cache_v, cache_len, global_row, slot_request, filled)
    returned = lax.all_to_all(
        attended.reshape(devices, capacity, width),
        ("req", "mlp"),
        split_axis=0,
        concat_axis=0,
        tiled=True,
    )
    attn_rows = jnp.dot(
        dispatch, returned.reshape(slot_count, width), preferred_element_type=jnp.float32
    ).astype(jnp.bfloat16)
    projected_out = jnp.dot(attn_rows, w_out, preferred_element_type=jnp.float32)
    normed = layer_norm(projected_out + tokens.astype(jnp.float32), ln1_gain, ln1_bias).astype(
        jnp.bfloat16
    )
    gathered = lax.all_gather(normed, "mlp", axis=0, tiled=True)
    hidden = jax.nn.gelu(
        jnp.dot(gathered, w_fc1, preferred_element_type=jnp.float32), approximate=False
    ).astype(jnp.bfloat16)
    summed = lax.psum_scatter(
        jnp.dot(hidden, w_fc2, preferred_element_type=jnp.float32).astype(jnp.bfloat16),
        "mlp",
        scatter_dimension=0,
        tiled=True,
    ).astype(jnp.float32)
    return layer_norm(normed.astype(jnp.float32) + summed, ln2_gain, ln2_bias).astype(jnp.bfloat16)


def solution(mesh):
    placed = (
        P(("req", "mlp"), None),
        P(),
        P(),
        P(("req", "mlp")),
        P(("req", "mlp"), None, None),
        P(("req", "mlp"), None, None),
        P(),
        P(),
        P(None, "mlp"),
        P("mlp", None),
        P(),
        P(),
        P(),
        P(),
    )
    return jax.shard_map(
        per_device, mesh=mesh, in_specs=placed, out_specs=P(("req", "mlp"), None), check_vma=False
    )
```

profile of v0, /device:TPU:0, one launch (start us, length us, event | category | flops | bytes accessed | tf_op | source)
XLA Modules:
  0.0 244.5 jit_solution(8810175562565531426)
XLA Ops:
  10.8 11.1 %all-to-all-start = ((bf16[128,2,1024]{2,1,0:T(2,128)(2,1)}), bf16[128,2,1024]{2,1,0:T(2,128)(2,1)S(1)}, u32[]{:S(2)}, u32[]{:S(2)}) async-start(bf16[128,2,1024]{2,1,0:T(2,128)(2,1)} %reshape.262), calls=%async_computation | async-start | bytes 1048576 | tf_op jit(solution)/shard_map/all_to_all | solution.py:130
  23.7 12.0 %all-to-all-done = bf16[128,2,1024]{2,1,0:T(2,128)(2,1)S(1)} async-done(((bf16[128,2,1024]{2,1,0:T(2,128)(2,1)}), bf16[128,2,1024]{2,1,0:T(2,128)(2,1)S(1)}, u32[]{:S(2)}, u32[]{:S(2)}) %all-to-all-start) | async-done | bytes 524320 | tf_op jit(solution)/shard_map/all_to_all | solution.py:130
  35.9 4.6 %convolution_convert_fusion = bf16[256,3072]{1,0:T(8,128)(2,1)S(1)} fusion(bf16[256,1024]{1,0:T(8,128)(2,1)S(1)} %reshape.263, bf16[1024,3072]{1,0:T(8,128)(2,1)} %param.22), kind=kOutput, calls=%fused_computation.18 | convolution fusion | flops 1611399168 | bytes 8388608 | tf_op jit(solution)/shard_map/dot_general | solution.py:137
  42.7 4.1 %fusion.8 = (f32[16,256]{1,0:T(8,128)S(1)}, f32[16,256,256]{1,2,0:T(8,128)}) fusion(pred[256,256]{0,1:T(8,128)(4,1)S(1)} %compare_and_fusion, bf16[256,16,64]{0,2,1:T(8,128)(2,1)} %bitcast.82, bf16[256,16,64]{0,2,1:T(8,128)(2,1)S(1)} %bitcast.85), kind=kOutput, calls=%fused_computation.19 | convolution fusion | flops 137359360 | bytes 5324800 | tf_op jit(solution)/shard_map/rhd,shd->hrs/dot_general | solution.py:49
  46.7 88.6 %while.13 = (s32[]{:T(128)}, f32[4,256,16,64]{1,3,2,0:T(8,128)}, f32[4,16,256]{2,1,0:T(8,128)S(1)}, bf16[4,512,1024]{2,1,0:T(8,128)(2,1)}, s32[4]{0:T(128)S(1)},...) while((s32[]{:T(128)}, f32[4,256,16,64]{1,3,2,0:T(8,128)}, ...), condition=%wide.region_9.10_spmd.clone, body=%wide.region_7.9_spmd.clone.sunk | while | flops 551691008 | bytes 29347476 | solution.py:82
  49.3 2.7 %constant_dynamic-slice_fusion.4 = (bf16[1,512,1024]{2,1,0:T(8,128)(2,1)}, bf16[1,512,1024]{2,1,0:T(8,128)(2,1)S(1)}) fusion(bf16[4,512,1024]{2,1,0:T(8,128)(2,1)} %get-tuple-element.249, s32[]{:T(128)} %get-tuple-element.231, bf16[4,512,1024]{2,1,0:T(8,128)(2,1)} %get-tuple-element.245), kind=kLoop, calls=%fused_computation.12.clone.1 | loop fusion | bytes 4194308 | tf_op jit(solution)/shard_map/while/body/jit(dynamic_index_in_dim)/dynamic_slice | solution.py:82
  54.3 6.5 %fusion.122 = (f32[16,256]{1,0:T(8,128)S(1)}, f32[16,512,256]{2,1,0:T(8,128)}) fusion(pred[256,512]{0,1:T(8,128)(4,1)S(1)} %broadcast_and_fusion.2, bf16[512,16,64]{0,2,1:T(8,128)(2,1)} %bitcast.79, bf16[256,16,64]{0,2,1:T(8,128)(2,1)} %get-tuple-element.250), kind=kOutput, calls=%fused_computation.3.clone.1 | convolution fusion | flops 274722816 | bytes 10108928 | tf_op jit(solution)/shard_map/while/body/eval_jaxpr/rhd,khd->hrk/dot_general | solution.py:60
  62.2 6.7 %fusion.123 = f32[4,256,16,64]{1,3,2,0:T(8,128)} fusion(f32[4,256,16,64]{1,3,2,0:T(8,128)} %get-tuple-element.232, s32[]{:T(128)} %get-tuple-element.231, bf16[512,16,64]{0,2,1:T(8,128)(2,1)} %bitcast.78, f32[16,512,256]{2,1,0:T(8,128)} %get-tuple-element.218, f32[16,256]{1,0:T(8,128)S(1)} %compare_select_fusion.3, ...), kind=kOutput, calls=%fused_computation.6.clone.1 | convolution fusion | flops 276824064 | bytes 10633728 | tf_op jit(solution)/shard_map/while/body/eval_jaxpr/hrk,khd->rhd/dot_general | solution.py:73
  71.6 2.7 %constant_dynamic-slice_fusion.4 = (bf16[1,512,1024]{2,1,0:T(8,128)(2,1)}, bf16[1,512,1024]{2,1,0:T(8,128)(2,1)S(1)}) fusion(bf16[4,512,1024]{2,1,0:T(8,128)(2,1)} %get-tuple-element.249, s32[]{:T(128)} %get-tuple-element.231, bf16[4,512,1024]{2,1,0:T(8,128)(2,1)} %get-tuple-element.245), kind=kLoop, calls=%fused_computation.12.clone.1 | loop fusion | bytes 4194308 | tf_op jit(solution)/shard_map/while/body/jit(dynamic_index_in_dim)/dynamic_slice | solution.py:82
  74.3 2.3 copy.56
  76.6 6.5 %fusion.122 = (f32[16,256]{1,0:T(8,128)S(1)}, f32[16,512,256]{2,1,0:T(8,128)}) fusion(pred[256,512]{0,1:T(8,128)(4,1)S(1)} %broadcast_and_fusion.2, bf16[512,16,64]{0,2,1:T(8,128)(2,1)} %bitcast.79, bf16[256,16,64]{0,2,1:T(8,128)(2,1)} %get-tuple-element.250), kind=kOutput, calls=%fused_computation.3.clone.1 | convolution fusion | flops 274722816 | bytes 10108928 | tf_op jit(solution)/shard_map/while/body/eval_jaxpr/rhd,khd->hrk/dot_general | solution.py:60
  84.4 6.7 %fusion.123 = f32[4,256,16,64]{1,3,2,0:T(8,128)} fusion(f32[4,256,16,64]{1,3,2,0:T(8,128)} %get-tuple-element.232, s32[]{:T(128)} %get-tuple-element.231, bf16[512,16,64]{0,2,1:T(8,128)(2,1)} %bitcast.78, f32[16,512,256]{2,1,0:T(8,128)} %get-tuple-element.218, f32[16,256]{1,0:T(8,128)S(1)} %compare_select_fusion.3, ...), kind=kOutput, calls=%fused_computation.6.clone.1 | convolution fusion | flops 276824064 | bytes 10633728 | tf_op jit(solution)/shard_map/while/body/eval_jaxpr/hrk,khd->rhd/dot_general | solution.py:73
  93.7 2.7 %constant_dynamic-slice_fusion.4 = (bf16[1,512,1024]{2,1,0:T(8,128)(2,1)}, bf16[1,512,1024]{2,1,0:T(8,128)(2,1)S(1)}) fusion(bf16[4,512,1024]{2,1,0:T(8,128)(2,1)} %get-tuple-element.249, s32[]{:T(128)} %get-tuple-element.231, bf16[4,512,1024]{2,1,0:T(8,128)(2,1)} %get-tuple-element.245), kind=kLoop, calls=%fused_computation.12.clone.1 | loop fusion | bytes 4194308 | tf_op jit(solution)/shard_map/while/body/jit(dynamic_index_in_dim)/dynamic_slice | solution.py:82
  98.7 6.5 %fusion.122 = (f32[16,256]{1,0:T(8,128)S(1)}, f32[16,512,256]{2,1,0:T(8,128)}) fusion(pred[256,512]{0,1:T(8,128)(4,1)S(1)} %broadcast_and_fusion.2, bf16[512,16,64]{0,2,1:T(8,128)(2,1)} %bitcast.79, bf16[256,16,64]{0,2,1:T(8,128)(2,1)} %get-tuple-element.250), kind=kOutput, calls=%fused_computation.3.clone.1 | convolution fusion | flops 274722816 | bytes 10108928 | tf_op jit(solution)/shard_map/while/body/eval_jaxpr/rhd,khd->hrk/dot_general | solution.py:60
  106.5 6.7 %fusion.123 = f32[4,256,16,64]{1,3,2,0:T(8,128)} fusion(f32[4,256,16,64]{1,3,2,0:T(8,128)} %get-tuple-element.232, s32[]{:T(128)} %get-tuple-element.231, bf16[512,16,64]{0,2,1:T(8,128)(2,1)} %bitcast.78, f32[16,512,256]{2,1,0:T(8,128)} %get-tuple-element.218, f32[16,256]{1,0:T(8,128)S(1)} %compare_select_fusion.3, ...), kind=kOutput, calls=%fused_computation.6.clone.1 | convolution fusion | flops 276824064 | bytes 10633728 | tf_op jit(solution)/shard_map/while/body/eval_jaxpr/hrk,khd->rhd/dot_general | solution.py:73
  115.8 2.7 %constant_dynamic-slice_fusion.4 = (bf16[1,512,1024]{2,1,0:T(8,128)(2,1)}, bf16[1,512,1024]{2,1,0:T(8,128)(2,1)S(1)}) fusion(bf16[4,512,1024]{2,1,0:T(8,128)(2,1)} %get-tuple-element.249, s32[]{:T(128)} %get-tuple-element.231, bf16[4,512,1024]{2,1,0:T(8,128)(2,1)} %get-tuple-element.245), kind=kLoop, calls=%fused_computation.12.clone.1 | loop fusion | bytes 4194308 | tf_op jit(solution)/shard_map/while/body/jit(dynamic_index_in_dim)/dynamic_slice | solution.py:82
  120.8 6.5 %fusion.122 = (f32[16,256]{1,0:T(8,128)S(1)}, f32[16,512,256]{2,1,0:T(8,128)}) fusion(pred[256,512]{0,1:T(8,128)(4,1)S(1)} %broadcast_and_fusion.2, bf16[512,16,64]{0,2,1:T(8,128)(2,1)} %bitcast.79, bf16[256,16,64]{0,2,1:T(8,128)(2,1)} %get-tuple-element.250), kind=kOutput, calls=%fused_computation.3.clone.1 | convolution fusion | flops 274722816 | bytes 10108928 | tf_op jit(solution)/shard_map/while/body/eval_jaxpr/rhd,khd->hrk/dot_general | solution.py:60
  128.7 6.7 %fusion.123 = f32[4,256,16,64]{1,3,2,0:T(8,128)} fusion(f32[4,256,16,64]{1,3,2,0:T(8,128)} %get-tuple-element.232, s32[]{:T(128)} %get-tuple-element.231, bf16[512,16,64]{0,2,1:T(8,128)(2,1)} %bitcast.78, f32[16,512,256]{2,1,0:T(8,128)} %get-tuple-element.218, f32[16,256]{1,0:T(8,128)S(1)} %compare_select_fusion.3, ...), kind=kOutput, calls=%fused_computation.6.clone.1 | convolution fusion | flops 276824064 | bytes 10633728 | tf_op jit(solution)/shard_map/while/body/eval_jaxpr/hrk,khd->rhd/dot_general | solution.py:73
  135.4 3.7 %reduce_sum.116 = f32[256,16,64]{0,2,1:T(8,128)} reduce(f32[4,256,16,64]{1,3,2,0:T(8,128)} %get-tuple-element.63, f32[]{:T(128)} %constant.28.clone.1), dimensions={0}, to_apply=%region_10.11 | reduce | flops 786432 | bytes 5242884 | tf_op jit(solution)/shard_map/reduce_sum | solution.py:86
  139.3 4.4 %fusion.22 = bf16[256,16,64]{0,2,1:T(8,128)(2,1)} fusion(f32[256,16,64]{0,2,1:T(8,128)} %reduce_sum.116, bf16[256,16,64]{0,2,1:T(8,128)(2,1)S(1)} %bitcast.84, f32[16,256,256]{1,2,0:T(8,128)} %get-tuple-element.148, f32[16,256]{1,0:T(8,128)S(1)} %compare_select_fusion.1, pred[256,256]{0,1:T(8,128)(4,1)S(1)} %compare_and_fusion), kind=kOutput, calls=%fused_computation.43 | convolution fusion | flops 138936320 | bytes 6373376 | tf_op jit(solution)/shard_map/hrs,shd->rhd/dot_general | solution.py:87
  147.1 18.7 %all_to_all.10 = bf16[128,2,1024]{2,1,0:T(2,128)(2,1)S(1)} all-to-all(bf16[128,2,1024]{2,1,0:T(2,128)(2,1)} %convert_element_type.69), channel_id=1, replica_groups=mesh['req'=16,'mlp'=8] {'req','mlp'}, dimensions={0} | all-to-all | bytes 1048576 | tf_op jit(solution)/shard_map/all_to_all | solution.py:144
  167.9 21.2 %all-gather.2.cloned.1.call-done = bf16[1024,1024]{1,0:T(8,128)(2,1)} async-done(((bf16[128,1024]{1,0:T(8,128)(2,1)}), bf16[1024,1024]{1,0:T(8,128)(2,1)}) %all-gather.2.cloned.1.call-update) | async-done | bytes 2097168 | tf_op jit(solution)/shard_map/all_gather | solution.py:158
  189.2 9.7 %convolution_convert_fusion.1 = bf16[1024,1024]{1,0:T(8,128)(2,1)} fusion(bf16[512,1024]{1,0:T(8,128)(2,1)} %param.25, bf16[1024,1024]{1,0:T(8,128)(2,1)} %all-gather.2.cloned.1.call-done, bf16[1024,512]{1,0:T(8,128)(2,1)} %param.24), kind=kOutput, calls=%fused_computation.40 | convolution fusion | flops 2182610944 | bytes 6291456 | tf_op jit(solution)/shard_map/dot_general | solution.py:163
  198.9 34.3 %reduce-scatter.2.cloned.1.call-done = bf16[128,1024]{1,0:T(8,128)(2,1)} async-done(((bf16[1024,1024]{1,0:T(8,128)(2,1)}), bf16[128,1024]{1,0:T(8,128)(2,1)}) %reduce-scatter.2.cloned.1.call-update) | async-done | bytes 262160 | tf_op jit(solution)/shard_map/reduce_scatter | solution.py:162
  (110 shorter events, 40.9 us)
Async XLA Ops:
  6.5 159.5 %copy-start = (bf16[1024,1024]{1,0:T(8,128)(2,1)S(1)}, bf16[1024,1024]{1,0:T(8,128)(2,1)}, u32[]{:S(2)}) copy-start(bf16[1024,1024]{1,0:T(8,128)(2,1)} %param.23) | copy-start | bytes 6291460
  6.5 15.5 %copy-start.3 = (s32[16384,1]{0,1:T(1,128)S(1)}, s32[16384,1]{0,1:T(1,128)}, u32[]{:S(2)}) copy-start(s32[16384,1]{0,1:T(1,128)} %param.17) | copy-start | bytes 196612
  6.5 15.9 %copy-start.6 = (s32[16384]{0:T(1024)S(1)}, s32[16384]{0:T(1024)}, u32[]{:S(2)}) copy-start(s32[16384]{0:T(1024)} %param.18) | copy-start | bytes 196612
  10.8 24.9 %all-to-all-start = ((bf16[128,2,1024]{2,1,0:T(2,128)(2,1)}), bf16[128,2,1024]{2,1,0:T(2,128)(2,1)S(1)}, u32[]{:S(2)}, u32[]{:S(2)}) async-start(bf16[128,2,1024]{2,1,0:T(2,128)(2,1)} %reshape.262), calls=%async_computation | async-start | bytes 1048576 | tf_op jit(solution)/shard_map/all_to_all | solution.py:130
  21.9 167.2 %all-gather.2.cloned.1.call-start = ((), (), s32[]{:S(2)}) async-start(), calls=%async_computation.3 | async-start | bytes 2359296 | tf_op jit(solution)/shard_map/all_gather | solution.py:158
  42.6 4.1 %copy-start.9 = (s32[4]{0:T(128)S(1)}, s32[4]{0:T(128)}, u32[]{:S(2)}) copy-start(s32[4]{0:T(128)} %param.19) | copy-start | bytes 52
  135.4 3.7 %copy-start.1 = (bf16[256,1024]{1,0:T(8,128)(2,1)S(1)}, bf16[256,1024]{1,0:T(8,128)(2,1)}, u32[]{:S(2)}) copy-start(bf16[256,1024]{1,0:T(8,128)(2,1)} %get-tuple-element.144) | copy-start | bytes 1572868
  145.7 20.3 %copy-start.2 = (bf16[128,1024]{1,0:T(8,128)(2,1)S(1)}, bf16[128,1024]{1,0:T(8,128)(2,1)}, u32[]{:S(2)}) copy-start(bf16[128,1024]{1,0:T(8,128)(2,1)} %param.16) | copy-start | bytes 786436
  166.0 0.9 copy-start.4
  166.0 0.9 copy-start.5
  167.9 65.3 %reduce-scatter.2.cloned.1.call-start = ((), (), s32[]{:S(2)}) async-start(), calls=%async_computation.4 | async-start | bytes 2359296 | tf_op jit(solution)/shard_map/reduce_scatter | solution.py:162
  198.8 36.8 %copy-start.7 = (f32[1024]{0:T(1024)S(1)}, f32[1024]{0:T(1024)}, u32[]{:S(2)}) copy-start(f32[1024]{0:T(1024)} %param.29) | copy-start | bytes 12292
  198.8 36.8 %copy-start.8 = (f32[1024]{0:T(1024)S(1)}, f32[1024]{0:T(1024)}, u32[]{:S(2)}) copy-start(f32[1024]{0:T(1024)} %param.28) | copy-start | bytes 12292
Sparse Core Ops, SparseCore 0:
  168.0 21.1 all-gather.1
  199.0 34.1 reduce-scatter.1
where the time goes:
time: 245 us; the launch traced here: 244 us
  matrix products  77.6 us (32%)
  waiting for transfers between devices  67.5 us (28%)
  local copies, waits for them, and re-layouts  39.5 us (16%)
  blocking collectives  18.7 us (8%)
  other arithmetic  16 us (7%)
  between operations  13.7 us (6%)
  starting transfers between devices  11.2 us (5%)
    reduce_scatter x1, waiting for transfers between devices, per_device(): lax.psum_scatter(jnp.dot(hidden, w_fc2, preferred_element_type=jnp.float3...  34.3 us
    dynamic_slice x20, local copies, waits for them, and re-layouts, attend(): lax.map(one_request, (cache_keys, cache_values, lengths, request_ids))  30 us
    dot_general x4, matrix products, one_request(): jnp.einsum('hrk,khd->rhd', weight, values_here.reshape(context, HEADS, he...  26.8 us
    dot_general x4, matrix products, one_request(): jnp.einsum('rhd,khd->hrk', queries, keys_here.reshape(context, HEADS, hea...  26.1 us
    all_gather x1, waiting for transfers between devices, per_device(): gathered = lax.all_gather(normed, 'mlp', axis=0, tiled=True)  21.2 us
    all_to_all x1, blocking collectives, per_device(): lax.all_to_all(attended.reshape(devices, capacity, width), ('req', 'mlp')...  18.7 us
    all_to_all x1, waiting for transfers between devices, per_device(): lax.all_to_all(outgoing.reshape(devices, capacity, width), ('req', 'mlp')...  12 us
    all_to_all x1, starting transfers between devices, per_device(): lax.all_to_all(outgoing.reshape(devices, capacity, width), ('req', 'mlp')...  11.1 us
  transfers between devices with their start and end apart: 3, of which 3 were waited for; matrix products, arithmetic and copies ran while one was open for 1% of the time, Pallas kernels for 0%

commit v1 on v0

--- a/solution.py
+++ b/solution.py
@@ -155,7 +155,23 @@
     normed = layer_norm(projected_out + tokens.astype(jnp.float32), ln1_gain, ln1_bias).astype(
         jnp.bfloat16
     )
-    gathered = lax.all_gather(normed, "mlp", axis=0, tiled=True)
+    peers, position, width_2 = (lax.axis_size("mlp"), lax.axis_index("mlp"), normed.shape[0])
+    right = [(i, (i + 1) % peers) for i in range(peers)]
+    downward = [(i, (i - 1) % peers) for i in range(peers)]
+    gathered = jnp.zeros((*normed.shape[:0], peers * width_2, *normed.shape[0 + 1 :]), normed.dtype)
+    gathered = lax.dynamic_update_slice_in_dim(gathered, normed, position * width_2, axis=0)
+    from_left = from_right = normed
+    half = peers // 2
+    for step in range(1, half + 1):
+        from_left = lax.ppermute(from_left, "mlp", right)
+        gathered = lax.dynamic_update_slice_in_dim(
+            gathered, from_left, (position - step) % peers * width_2, axis=0
+        )
+        if step < peers - half:
+            from_right = lax.ppermute(from_right, "mlp", downward)
+            gathered = lax.dynamic_update_slice_in_dim(
+                gathered, from_right, (position + step) % peers * width_2, axis=0
+            )
     hidden = jax.nn.gelu(
         jnp.dot(gathered, w_fc1, preferred_element_type=jnp.float32), approximate=False
     ).astype(jnp.bfloat16)

time: 245 us -> 246 us (level)
  blocking collectives: 18.7 us -> 0 us
  starting transfers between devices: 11.2 us -> 24.9 us
  local copies, waits for them, and re-layouts: 39.5 us -> 45.1 us
    all_gather x1 -> x0, waiting for transfers between devices: 21.2 us -> none  [per_device(): gathered = lax.all_gather(normed, 'mlp', axis=0, tiled=True)]
    all_to_all x1 -> x0, blocking collectives: 18.7 us -> none  [per_device(): lax.all_to_all(attended.reshape(devices, capacity, width), ('req', 'mlp')...]
    ppermute x0 -> x7, waiting for transfers between devices: none -> 14.8 us  [the longest x4 14.8 us: per_device(): from_left = lax.ppermute(from_left, 'mlp', right)]
    all_to_all x0 -> x1, waiting for transfers between devices: none -> 13.7 us  [per_device(): lax.all_to_all(attended.reshape(devices, capacity, width), ('req', 'mlp')...]
    ppermute x0 -> x7, starting transfers between devices: none -> 8.88 us  [the longest x3 8.86 us: per_device(): from_right = lax.ppermute(from_right, 'mlp', downward)]
    reduce_scatter x1, waiting for transfers between devices: 34.3 us -> 28.5 us  [per_device(): lax.psum_scatter(jnp.dot(hidden, w_fc2, preferred_element_type=jnp.float3...]
    dynamic_update_slice x0 -> x7, local copies, waits for them, and re-layouts: none -> 5.08 us  [the longest x4 2.9 us: per_device(): lax.dynamic_update_slice_in_dim(gathered, from_left, (position - step) %...]
    all_to_all x0 -> x1, starting transfers between devices: none -> 4.79 us  [per_device(): lax.all_to_all(attended.reshape(devices, capacity, width), ('req', 'mlp')...]
  transfers between devices with their start and end apart: 3 -> 10, of which waited for: 3 -> 7; matrix products, arithmetic and copies ran while one was open for 1% -> 2% of each run, Pallas kernels for 0% -> 0%
where the time goes in v1:
time: 246 us; the launch traced here: 245 us
  matrix products  77.6 us (32%)
  waiting for transfers between devices  68.9 us (28%)
  local copies, waits for them, and re-layouts  45.1 us (18%)
  starting transfers between devices  24.9 us (10%)
  other arithmetic  14.9 us (6%)
  between operations  13.7 us (6%)
    dynamic_slice x20, local copies, waits for them, and re-layouts, attend(): lax.map(one_request, (cache_keys, cache_values, lengths, request_ids))  30 us
    reduce_scatter x1, waiting for transfers between devices, per_device(): lax.psum_scatter(jnp.dot(hidden, w_fc2, preferred_element_type=jnp.float3...  28.5 us
    dot_general x4, matrix products, one_request(): jnp.einsum('hrk,khd->rhd', weight, values_here.reshape(context, HEADS, he...  26.8 us
    dot_general x4, matrix products, one_request(): jnp.einsum('rhd,khd->hrk', queries, keys_here.reshape(context, HEADS, hea...  26.1 us
    ppermute x4, waiting for transfers between devices, per_device(): from_left = lax.ppermute(from_left, 'mlp', right)  14.8 us
    all_to_all x1, waiting for transfers between devices, per_device(): lax.all_to_all(attended.reshape(devices, capacity, width), ('req', 'mlp')...  13.7 us
    all_to_all x1, waiting for transfers between devices, per_device(): lax.all_to_all(outgoing.reshape(devices, capacity, width), ('req', 'mlp')...  12 us
    all_to_all x1, starting transfers between devices, per_device(): lax.all_to_all(outgoing.reshape(devices, capacity, width), ('req', 'mlp')...  11.1 us
  transfers between devices with their start and end apart: 10, of which 7 were waited for; matrix products, arithmetic and copies ran while one was open for 2% of the time, Pallas kernels for 0%

profile of v1, /device:TPU:0, one launch (start us, length us, event | category | flops | bytes accessed | tf_op | source)
XLA Modules:
  0.0 245.3 jit_solution(3995212513223911768)
XLA Ops:
  10.8 11.1 %all-to-all-start = ((bf16[128,2,1024]{2,1,0:T(2,128)(2,1)}), bf16[128,2,1024]{2,1,0:T(2,128)(2,1)S(1)}, u32[]{:S(2)}, u32[]{:S(2)}) async-start(bf16[128,2,1024]{2,1,0:T(2,128)(2,1)} %reshape.262), calls=%async_computation | async-start | bytes 1048576 | tf_op jit(solution)/shard_map/all_to_all | solution.py:130
  23.6 12.0 %all-to-all-done = bf16[128,2,1024]{2,1,0:T(2,128)(2,1)S(1)} async-done(((bf16[128,2,1024]{2,1,0:T(2,128)(2,1)}), bf16[128,2,1024]{2,1,0:T(2,128)(2,1)S(1)}, u32[]{:S(2)}, u32[]{:S(2)}) %all-to-all-start) | async-done | bytes 524320 | tf_op jit(solution)/shard_map/all_to_all | solution.py:130
  35.9 4.6 %convolution_convert_fusion = bf16[256,3072]{1,0:T(8,128)(2,1)S(1)} fusion(bf16[256,1024]{1,0:T(8,128)(2,1)S(1)} %reshape.263, bf16[1024,3072]{1,0:T(8,128)(2,1)} %param.22), kind=kOutput, calls=%fused_computation.18 | convolution fusion | flops 1611399168 | bytes 8388608 | tf_op jit(solution)/shard_map/dot_general | solution.py:137
  42.7 4.1 %fusion.8 = (f32[16,256]{1,0:T(8,128)S(1)}, f32[16,256,256]{1,2,0:T(8,128)}) fusion(pred[256,256]{0,1:T(8,128)(4,1)S(1)} %compare_and_fusion, bf16[256,16,64]{0,2,1:T(8,128)(2,1)} %bitcast.82, bf16[256,16,64]{0,2,1:T(8,128)(2,1)S(1)} %bitcast.85), kind=kOutput, calls=%fused_computation.19 | convolution fusion | flops 137359360 | bytes 5324800 | tf_op jit(solution)/shard_map/rhd,shd->hrs/dot_general | solution.py:49
  46.7 88.6 %while.13 = (s32[]{:T(128)}, f32[4,256,16,64]{1,3,2,0:T(8,128)}, f32[4,16,256]{2,1,0:T(8,128)S(1)}, bf16[4,512,1024]{2,1,0:T(8,128)(2,1)}, s32[4]{0:T(128)S(1)},...) while((s32[]{:T(128)}, f32[4,256,16,64]{1,3,2,0:T(8,128)}, ...), condition=%wide.region_9.10_spmd.clone, body=%wide.region_7.9_spmd.clone.sunk | while | flops 551691008 | bytes 29347476 | solution.py:82
  54.3 6.5 %fusion.122 = (f32[16,256]{1,0:T(8,128)S(1)}, f32[16,512,256]{2,1,0:T(8,128)}) fusion(pred[256,512]{0,1:T(8,128)(4,1)S(1)} %broadcast_and_fusion.2, bf16[512,16,64]{0,2,1:T(8,128)(2,1)} %bitcast.79, bf16[256,16,64]{0,2,1:T(8,128)(2,1)} %get-tuple-element.252), kind=kOutput, calls=%fused_computation.3.clone.1 | convolution fusion | flops 274722816 | bytes 10108928 | tf_op jit(solution)/shard_map/while/body/eval_jaxpr/rhd,khd->hrk/dot_general | solution.py:60
  62.2 6.7 %fusion.123 = f32[4,256,16,64]{1,3,2,0:T(8,128)} fusion(f32[4,256,16,64]{1,3,2,0:T(8,128)} %get-tuple-element.234, s32[]{:T(128)} %get-tuple-element.233, bf16[512,16,64]{0,2,1:T(8,128)(2,1)} %bitcast.78, f32[16,512,256]{2,1,0:T(8,128)} %get-tuple-element.220, f32[16,256]{1,0:T(8,128)S(1)} %compare_select_fusion.3, ...), kind=kOutput, calls=%fused_computation.6.clone.1 | convolution fusion | flops 276824064 | bytes 10633728 | tf_op jit(solution)/shard_map/while/body/eval_jaxpr/hrk,khd->rhd/dot_general | solution.py:73
  76.6 6.5 %fusion.122 = (f32[16,256]{1,0:T(8,128)S(1)}, f32[16,512,256]{2,1,0:T(8,128)}) fusion(pred[256,512]{0,1:T(8,128)(4,1)S(1)} %broadcast_and_fusion.2, bf16[512,16,64]{0,2,1:T(8,128)(2,1)} %bitcast.79, bf16[256,16,64]{0,2,1:T(8,128)(2,1)} %get-tuple-element.252), kind=kOutput, calls=%fused_computation.3.clone.1 | convolution fusion | flops 274722816 | bytes 10108928 | tf_op jit(solution)/shard_map/while/body/eval_jaxpr/rhd,khd->hrk/dot_general | solution.py:60
  84.4 6.7 %fusion.123 = f32[4,256,16,64]{1,3,2,0:T(8,128)} fusion(f32[4,256,16,64]{1,3,2,0:T(8,128)} %get-tuple-element.234, s32[]{:T(128)} %get-tuple-element.233, bf16[512,16,64]{0,2,1:T(8,128)(2,1)} %bitcast.78, f32[16,512,256]{2,1,0:T(8,128)} %get-tuple-element.220, f32[16,256]{1,0:T(8,128)S(1)} %compare_select_fusion.3, ...), kind=kOutput, calls=%fused_computation.6.clone.1 | convolution fusion | flops 276824064 | bytes 10633728 | tf_op jit(solution)/shard_map/while/body/eval_jaxpr/hrk,khd->rhd/dot_general | solution.py:73
  98.7 6.5 %fusion.122 = (f32[16,256]{1,0:T(8,128)S(1)}, f32[16,512,256]{2,1,0:T(8,128)}) fusion(pred[256,512]{0,1:T(8,128)(4,1)S(1)} %broadcast_and_fusion.2, bf16[512,16,64]{0,2,1:T(8,128)(2,1)} %bitcast.79, bf16[256,16,64]{0,2,1:T(8,128)(2,1)} %get-tuple-element.252), kind=kOutput, calls=%fused_computation.3.clone.1 | convolution fusion | flops 274722816 | bytes 10108928 | tf_op jit(solution)/shard_map/while/body/eval_jaxpr/rhd,khd->hrk/dot_general | solution.py:60
  106.5 6.7 %fusion.123 = f32[4,256,16,64]{1,3,2,0:T(8,128)} fusion(f32[4,256,16,64]{1,3,2,0:T(8,128)} %get-tuple-element.234, s32[]{:T(128)} %get-tuple-element.233, bf16[512,16,64]{0,2,1:T(8,128)(2,1)} %bitcast.78, f32[16,512,256]{2,1,0:T(8,128)} %get-tuple-element.220, f32[16,256]{1,0:T(8,128)S(1)} %compare_select_fusion.3, ...), kind=kOutput, calls=%fused_computation.6.clone.1 | convolution fusion | flops 276824064 | bytes 10633728 | tf_op jit(solution)/shard_map/while/body/eval_jaxpr/hrk,khd->rhd/dot_general | solution.py:73
  120.8 6.5 %fusion.122 = (f32[16,256]{1,0:T(8,128)S(1)}, f32[16,512,256]{2,1,0:T(8,128)}) fusion(pred[256,512]{0,1:T(8,128)(4,1)S(1)} %broadcast_and_fusion.2, bf16[512,16,64]{0,2,1:T(8,128)(2,1)} %bitcast.79, bf16[256,16,64]{0,2,1:T(8,128)(2,1)} %get-tuple-element.252), kind=kOutput, calls=%fused_computation.3.clone.1 | convolution fusion | flops 274722816 | bytes 10108928 | tf_op jit(solution)/shard_map/while/body/eval_jaxpr/rhd,khd->hrk/dot_general | solution.py:60
  128.7 6.7 %fusion.123 = f32[4,256,16,64]{1,3,2,0:T(8,128)} fusion(f32[4,256,16,64]{1,3,2,0:T(8,128)} %get-tuple-element.234, s32[]{:T(128)} %get-tuple-element.233, bf16[512,16,64]{0,2,1:T(8,128)(2,1)} %bitcast.78, f32[16,512,256]{2,1,0:T(8,128)} %get-tuple-element.220, f32[16,256]{1,0:T(8,128)S(1)} %compare_select_fusion.3, ...), kind=kOutput, calls=%fused_computation.6.clone.1 | convolution fusion | flops 276824064 | bytes 10633728 | tf_op jit(solution)/shard_map/while/body/eval_jaxpr/hrk,khd->rhd/dot_general | solution.py:73
  135.4 3.7 %reduce_sum.116 = f32[256,16,64]{0,2,1:T(8,128)} reduce(f32[4,256,16,64]{1,3,2,0:T(8,128)} %get-tuple-element.63, f32[]{:T(128)} %constant.140.clone.1), dimensions={0}, to_apply=%region_10.11 | reduce | flops 786432 | bytes 5242884 | tf_op jit(solution)/shard_map/reduce_sum | solution.py:86
  139.3 4.4 %fusion.22 = bf16[256,16,64]{0,2,1:T(8,128)(2,1)} fusion(f32[256,16,64]{0,2,1:T(8,128)} %reduce_sum.116, bf16[256,16,64]{0,2,1:T(8,128)(2,1)S(1)} %bitcast.84, f32[16,256,256]{1,2,0:T(8,128)} %get-tuple-element.150, f32[16,256]{1,0:T(8,128)S(1)} %compare_select_fusion.1, pred[256,256]{0,1:T(8,128)(4,1)S(1)} %compare_and_fusion), kind=kOutput, calls=%fused_computation.43 | convolution fusion | flops 138936320 | bytes 6373376 | tf_op jit(solution)/shard_map/hrs,shd->rhd/dot_general | solution.py:87
  147.1 4.8 %all-to-all-start.1 = ((bf16[128,2,1024]{2,1,0:T(2,128)(2,1)}), bf16[128,2,1024]{2,1,0:T(2,128)(2,1)S(1)}, u32[]{:S(2)}, u32[]{:S(2)}) async-start(bf16[128,2,1024]{2,1,0:T(2,128)(2,1)} %convert_element_type.69), calls=%async_computation.1 | async-start | bytes 1048576 | tf_op jit(solution)/shard_map/all_to_all | solution.py:144
  151.9 13.7 %all-to-all-done.1 = bf16[128,2,1024]{2,1,0:T(2,128)(2,1)S(1)} async-done(((bf16[128,2,1024]{2,1,0:T(2,128)(2,1)}), bf16[128,2,1024]{2,1,0:T(2,128)(2,1)S(1)}, u32[]{:S(2)}, u32[]{:S(2)}) %all-to-all-start.1) | async-done | bytes 524320 | tf_op jit(solution)/shard_map/all_to_all | solution.py:144
  170.4 4.1 %collective-permute-done = bf16[128,1024]{1,0:T(8,128)(2,1)S(1)} collective-permute-done((bf16[128,1024]{1,0:T(8,128)(2,1)S(1)}, bf16[128,1024]{1,0:T(8,128)(2,1)S(1)}, u32[]{:S(2)}, u32[]{:S(2)}) %collective-permute-start) | collective-permute-done | bytes 262176 | tf_op jit(solution)/shard_map/ppermute | solution.py:166
  174.4 3.0 %collective-permute-start.3 = (bf16[128,1024]{1,0:T(8,128)(2,1)S(1)}, bf16[128,1024]{1,0:T(8,128)(2,1)S(1)}, u32[]{:S(2)}, u32[]{:S(2)}) collective-permute-start(bf16[128,1024]{1,0:T(8,128)(2,1)S(1)} %collective-permute-done.1), channel_id=1, source_target_pairs={{0,7},{1,0},{2,1},{3,2},{4,3},{5,4},{6,5},{7,6},{8,15},{9,8},{10,9... | collective-permute-start | bytes 786440 | tf_op jit(solution)/shard_map/ppermute | solution.py:171
  177.4 4.0 %collective-permute-done.2 = bf16[128,1024]{1,0:T(8,128)(2,1)S(1)} collective-permute-done((bf16[128,1024]{1,0:T(8,128)(2,1)S(1)}, bf16[128,1024]{1,0:T(8,128)(2,1)S(1)}, u32[]{:S(2)}, u32[]{:S(2)}) %collective-permute-start.2) | collective-permute-done | bytes 262176 | tf_op jit(solution)/shard_map/ppermute | solution.py:166
  182.9 3.0 %collective-permute-start.5 = (bf16[128,1024]{1,0:T(8,128)(2,1)S(1)}, bf16[128,1024]{1,0:T(8,128)(2,1)S(1)}, u32[]{:S(2)}, u32[]{:S(2)}) collective-permute-start(bf16[128,1024]{1,0:T(8,128)(2,1)S(1)} %collective-permute-done.3), channel_id=1, source_target_pairs={{0,7},{1,0},{2,1},{3,2},{4,3},{5,4},{6,5},{7,6},{8,15},{9,8},{10,9... | collective-permute-start | bytes 786440 | tf_op jit(solution)/shard_map/ppermute | solution.py:171
  190.6 4.8 %collective-permute-done.6 = bf16[128,1024]{1,0:T(8,128)(2,1)S(1)} collective-permute-done((bf16[128,1024]{1,0:T(8,128)(2,1)S(1)}, bf16[128,1024]{1,0:T(8,128)(2,1)S(1)}, u32[]{:S(2)}, u32[]{:S(2)}) %collective-permute-start.6) | collective-permute-done | bytes 262176 | tf_op jit(solution)/shard_map/ppermute | solution.py:166
  196.2 9.7 %convolution_convert_fusion.1 = bf16[1024,1024]{1,0:T(8,128)(2,1)} fusion(bf16[512,1024]{1,0:T(8,128)(2,1)} %param.25, bf16[1024,1024]{1,0:T(8,128)(2,1)} %constant_dynamic-update-slice_fusion.7, bf16[1024,512]{1,0:T(8,128)(2,1)} %param.24), kind=kOutput, calls=%fused_computation.40 | convolution fusion | flops 2182610944 | bytes 6291456 | tf_op jit(solution)/shard_map/dot_general | solution.py:179
  205.9 28.5 %reduce-scatter.2.cloned.1.call-done = bf16[128,1024]{1,0:T(8,128)(2,1)} async-done(((bf16[1024,1024]{1,0:T(8,128)(2,1)}), bf16[128,1024]{1,0:T(8,128)(2,1)}) %reduce-scatter.2.cloned.1.call-update) | async-done | bytes 262160 | tf_op jit(solution)/shard_map/reduce_scatter | solution.py:178
  (132 shorter events, 63.3 us)
Async XLA Ops:
  6.5 159.2 %copy-start = (bf16[1024,1024]{1,0:T(8,128)(2,1)S(1)}, bf16[1024,1024]{1,0:T(8,128)(2,1)}, u32[]{:S(2)}) copy-start(bf16[1024,1024]{1,0:T(8,128)(2,1)} %param.23) | copy-start | bytes 6291460
  6.5 15.4 %copy-start.4 = (s32[16384,1]{0,1:T(1,128)S(1)}, s32[16384,1]{0,1:T(1,128)}, u32[]{:S(2)}) copy-start(s32[16384,1]{0,1:T(1,128)} %param.17) | copy-start | bytes 196612
  6.5 15.9 %copy-start.5 = (s32[16384]{0:T(1024)S(1)}, s32[16384]{0:T(1024)}, u32[]{:S(2)}) copy-start(s32[16384]{0:T(1024)} %param.18) | copy-start | bytes 196612
  10.8 24.9 %all-to-all-start = ((bf16[128,2,1024]{2,1,0:T(2,128)(2,1)}), bf16[128,2,1024]{2,1,0:T(2,128)(2,1)S(1)}, u32[]{:S(2)}, u32[]{:S(2)}) async-start(bf16[128,2,1024]{2,1,0:T(2,128)(2,1)} %reshape.262), calls=%async_computation | async-start | bytes 1048576 | tf_op jit(solution)/shard_map/all_to_all | solution.py:130
  42.6 4.1 %copy-start.10 = (s32[4]{0:T(128)S(1)}, s32[4]{0:T(128)}, u32[]{:S(2)}) copy-start(s32[4]{0:T(128)} %param.19) | copy-start | bytes 52
  135.4 3.7 %copy-start.2 = (bf16[256,1024]{1,0:T(8,128)(2,1)S(1)}, bf16[256,1024]{1,0:T(8,128)(2,1)}, u32[]{:S(2)}) copy-start(bf16[256,1024]{1,0:T(8,128)(2,1)} %get-tuple-element.146) | copy-start | bytes 1572868
  145.7 20.1 %copy-start.3 = (bf16[128,1024]{1,0:T(8,128)(2,1)S(1)}, bf16[128,1024]{1,0:T(8,128)(2,1)}, u32[]{:S(2)}) copy-start(bf16[128,1024]{1,0:T(8,128)(2,1)} %param.16) | copy-start | bytes 786436
  147.1 18.5 %all-to-all-start.1 = ((bf16[128,2,1024]{2,1,0:T(2,128)(2,1)}), bf16[128,2,1024]{2,1,0:T(2,128)(2,1)S(1)}, u32[]{:S(2)}, u32[]{:S(2)}) async-start(bf16[128,2,1024]{2,1,0:T(2,128)(2,1)} %convert_element_type.69), calls=%async_computation.1 | async-start | bytes 1048576 | tf_op jit(solution)/shard_map/all_to_all | solution.py:144
  151.9 82.5 %reduce-scatter.2.cloned.1.call-start = ((), (), s32[]{:S(2)}) async-start(), calls=%async_computation.3 | async-start | bytes 2359296 | tf_op jit(solution)/shard_map/reduce_scatter | solution.py:178
  166.5 0.7 copy-start.6
  166.5 0.7 copy-start.7
  167.4 7.0 %copy-start.1 = (bf16[1024,1024]{1,0:T(8,128)(2,1)}, bf16[1024,1024]{1,0:T(8,128)(2,1)S(1)}, u32[]{:S(2)}) copy-start(bf16[1024,1024]{1,0:T(8,128)(2,1)S(1)} %get-tuple-element.140) | copy-start | bytes 6291460
  167.4 7.0 %collective-permute-start = (bf16[128,1024]{1,0:T(8,128)(2,1)S(1)}, bf16[128,1024]{1,0:T(8,128)(2,1)S(1)}, u32[]{:S(2)}, u32[]{:S(2)}) collective-permute-start(bf16[128,1024]{1,0:T(8,128)(2,1)S(1)} %get-tuple-element.141), channel_id=1, source_target_pairs={{0,1},{1,2},{2,3},{3,4},{4,5},{5,6},{6,7},{7,0},{8,9},{9,10},{10,1... | collective-permute-start | bytes 786440 | tf_op jit(solution)/shard_map/ppermute | solution.py:166
  167.4 7.0 %collective-permute-start.1 = (bf16[128,1024]{1,0:T(8,128)(2,1)S(1)}, bf16[128,1024]{1,0:T(8,128)(2,1)S(1)}, u32[]{:S(2)}, u32[]{:S(2)}) collective-permute-start(bf16[128,1024]{1,0:T(8,128)(2,1)S(1)} %get-tuple-element.141), channel_id=1, source_target_pairs={{0,7},{1,0},{2,1},{3,2},{4,3},{5,4},{6,5},{7,6},{8,15},{9,8},{10,9... | collective-permute-start | bytes 786440 | tf_op jit(solution)/shard_map/ppermute | solution.py:171
  174.4 7.0 %collective-permute-start.2 = (bf16[128,1024]{1,0:T(8,128)(2,1)S(1)}, bf16[128,1024]{1,0:T(8,128)(2,1)S(1)}, u32[]{:S(2)}, u32[]{:S(2)}) collective-permute-start(bf16[128,1024]{1,0:T(8,128)(2,1)S(1)} %collective-permute-done), channel_id=1, source_target_pairs={{0,1},{1,2},{2,3},{3,4},{4,5},{5,6},{6,7},{7,0},{8,9},{9,10},{10,1... | collective-permute-start | bytes 786440 | tf_op jit(solution)/shard_map/ppermute | solution.py:166
  174.4 8.4 %collective-permute-start.3 = (bf16[128,1024]{1,0:T(8,128)(2,1)S(1)}, bf16[128,1024]{1,0:T(8,128)(2,1)S(1)}, u32[]{:S(2)}, u32[]{:S(2)}) collective-permute-start(bf16[128,1024]{1,0:T(8,128)(2,1)S(1)} %collective-permute-done.1), channel_id=1, source_target_pairs={{0,7},{1,0},{2,1},{3,2},{4,3},{5,4},{6,5},{7,6},{8,15},{9,8},{10,9... | collective-permute-start | bytes 786440 | tf_op jit(solution)/shard_map/ppermute | solution.py:171
  181.4 7.0 %collective-permute-start.4 = (bf16[128,1024]{1,0:T(8,128)(2,1)S(1)}, bf16[128,1024]{1,0:T(8,128)(2,1)S(1)}, u32[]{:S(2)}, u32[]{:S(2)}) collective-permute-start(bf16[128,1024]{1,0:T(8,128)(2,1)S(1)} %collective-permute-done.2), channel_id=1, source_target_pairs={{0,1},{1,2},{2,3},{3,4},{4,5},{5,6},{6,7},{7,0},{8,9},{9,10},{10,1... | collective-permute-start | bytes 786440 | tf_op jit(solution)/shard_map/ppermute | solution.py:166
  182.9 7.0 %collective-permute-start.5 = (bf16[128,1024]{1,0:T(8,128)(2,1)S(1)}, bf16[128,1024]{1,0:T(8,128)(2,1)S(1)}, u32[]{:S(2)}, u32[]{:S(2)}) collective-permute-start(bf16[128,1024]{1,0:T(8,128)(2,1)S(1)} %collective-permute-done.3), channel_id=1, source_target_pairs={{0,7},{1,0},{2,1},{3,2},{4,3},{5,4},{6,5},{7,6},{8,15},{9,8},{10,9... | collective-permute-start | bytes 786440 | tf_op jit(solution)/shard_map/ppermute | solution.py:171
  188.4 7.0 %collective-permute-start.6 = (bf16[128,1024]{1,0:T(8,128)(2,1)S(1)}, bf16[128,1024]{1,0:T(8,128)(2,1)S(1)}, u32[]{:S(2)}, u32[]{:S(2)}) collective-permute-start(bf16[128,1024]{1,0:T(8,128)(2,1)S(1)} %collective-permute-done.4), channel_id=1, source_target_pairs={{0,1},{1,2},{2,3},{3,4},{4,5},{5,6},{6,7},{7,0},{8,9},{9,10},{10,1... | collective-permute-start | bytes 786440 | tf_op jit(solution)/shard_map/ppermute | solution.py:166
  205.8 30.8 %copy-start.8 = (f32[1024]{0:T(1024)S(1)}, f32[1024]{0:T(1024)}, u32[]{:S(2)}) copy-start(f32[1024]{0:T(1024)} %param.29) | copy-start | bytes 12292
  205.8 30.8 %copy-start.9 = (f32[1024]{0:T(1024)S(1)}, f32[1024]{0:T(1024)}, u32[]{:S(2)}) copy-start(f32[1024]{0:T(1024)} %param.28) | copy-start | bytes 12292
Sparse Core Ops, SparseCore 0:
  206.0 28.2 reduce-scatter.1
